TPU v7x, 256 devices: a whole 4x4x8 slice. The times are simulated.
256 devices in a mesh: freq: 4 (over y), mx: 8 (over x, core), my: 8 (over z).
Axes of the slice: x: 4, y: 4, z: 8, core: 2. Of those that a mesh axis runs over, the one named last changes fastest.
Arguments:
- adjoint_rhs: float32 [4, 2, 3, 512, 2048], P('freq', None, None, 'mx', 'my'), may hold values from -4 to 6
- state: bfloat16 [4, 2, 3, 512, 2048], P('freq', None, None, 'mx', 'my'), may hold values from -1.5 to 1.5
- density: float32 [512, 2048], P('mx', 'my'), may hold values from 0.85 to 1
- stiffness: float32 [512, 2048], P('mx', 'my'), may hold values from 1.5 to 4
- mass: float32 [512, 2048], P('mx', 'my'), may hold values from 0.2 to 1
- omega: float32 [4], P('freq'), may hold values from 0.15 to 0.45
- send_rows: int32 [64, 2048], P(('mx', 'my')), may hold values from 0 to 16383, as said below
- recv_rows: int32 [64, 2048], P(('mx', 'my')), may hold values from 0 to 16383, as said below
- mortar_weight: float32 [64, 2048], P(('mx', 'my')), may hold values from 0 to 1.5, as said below
Outputs:
- adjoint: float32 [4, 2, 3, 512, 2048], P('freq', None, None, 'mx', 'my')
- filtered_sensitivity: float32 [512, 2048], P('mx', 'my')
Inputs may be any that keep to these rules, and one draw needn't show every extreme that they name: `send_rows`: a local cell of the sending device; slots past the live count of a device pair hold 0. `recv_rows`: a local cell of the receiving device; empty slots hold 0. Live slots of a pair come first, up to 32 of them. `mortar_weight`: zero exactly in empty slots, at least 0.5 in live ones; every receiving device has a source device with all 32 slots live.
All inputs are finite; a program needn't handle non-finite values.
Results may differ from a plain program's by a relative error of at most 0.0003.
Values may be sent and summed in bfloat16 or wider, within the bound.
A program may use at most 64 MiB of HBM per device.

v0:
```python
import jax
import jax.numpy as jnp
from jax import lax
from jax.sharding import PartitionSpec as P

ITERS = 20


def extended(x, sides, width):
    for axis, dim in sides:
        size, length = (lax.axis_size(axis), x.shape[dim])
        up = [(i, (i + 1) % size) for i in range(size - 1)]
        down = [(j, i) for i, j in up]
        last = lax.slice_in_dim(x, length - width, length, axis=dim)
        first = lax.slice_in_dim(x, 0, width, axis=dim)
        before = lax.ppermute(last, axis, up)
        after = lax.ppermute(first, axis, down)
        x = jnp.concatenate([before, x, after], axis=dim)
    return x


def on_device(
    adjoint_rhs, state, density, stiffness, mass, omega, send_rows, recv_rows, mortar_weight
):
    rows_x, rows_y = density.shape
    cells = rows_x * rows_y
    w = omega[0]
    stiff = density**3 * stiffness
    dstiff = 3.0 * density**2 * stiffness
    rmass = density * mass
    sources = send_rows[0]
    targets = recv_rows[0]
    weights = mortar_weight[0]
    mdiag = jnp.zeros((cells,), jnp.float32).at[targets].add(weights).reshape(rows_x, rows_y)
    real_d = 4.4 * stiff + 0.3 + mdiag - w * w * rmass
    imag_d = 0.2 * w * (stiff + rmass)
    den = real_d * real_d + imag_d * imag_d
    rhs = adjoint_rhs.reshape(6, rows_x, rows_y)

    def mortar(field):
        sent = field.reshape(6, cells)[:, sources]
        got = lax.all_to_all(sent, ("mx", "my"), split_axis=1, concat_axis=1, tiled=True)
        added = jnp.zeros((6, cells), jnp.float32).at[:, targets].add(got * weights)
        return added.reshape(6, rows_x, rows_y)

    def sweep(step, field):
        padded = extended(field, (("mx", 1), ("my", 2)), 1)
        beside = (
            padded[:, 2:, 1:-1] + padded[:, :-2, 1:-1] + padded[:, 1:-1, 2:] + padded[:, 1:-1, :-2]
        )
        h = rhs + stiff * beside + mortar(field)
        new_re = (h[:3] * real_d + h[3:] * imag_d) / den
        new_im = (h[3:] * real_d - h[:3] * imag_d) / den
        return jnp.concatenate([new_re, new_im], axis=0)

    field = lax.fori_loop(0, ITERS, sweep, jnp.zeros((6, rows_x, rows_y), jnp.float32))
    state_six = state.reshape(6, rows_x, rows_y)
    state_pad = extended(state_six, (("mx", 1), ("my", 2)), 1).astype(jnp.float32)
    u = state_six.astype(jnp.float32)
    nb = (
        state_pad[:, 2:, 1:-1]
        + state_pad[:, :-2, 1:-1]
        + state_pad[:, 1:-1, 2:]
        + state_pad[:, 1:-1, :-2]
    )
    da = 4.4 * dstiff - w * w * mass
    db = 0.2 * w * (dstiff + mass)
    t_re = da * u[:3] - db * u[3:] - dstiff * nb[:3]
    t_im = da * u[3:] + db * u[:3] - dstiff * nb[3:]
    sens = -jnp.sum(field[:3] * t_re - field[3:] * t_im, axis=0)
    total = lax.psum(sens, "freq")
    weighted = extended(density * total, (("mx", 0), ("my", 1)), 1)
    filt = weighted[1:-1, 1:-1]
    filt = filt + 0.5 * (
        weighted[2:, 1:-1] + weighted[:-2, 1:-1] + weighted[1:-1, 2:] + weighted[1:-1, :-2]
    )
    filt = filt + 0.25 * (
        weighted[2:, 2:] + weighted[:-2, :-2] + weighted[2:, :-2] + weighted[:-2, 2:]
    )
    return (field.reshape(1, 2, 3, rows_x, rows_y), filt / (4.0 * density))


def solution(mesh):
    return jax.shard_map(
        on_device,
        mesh=mesh,
        in_specs=(
            P("freq", None, None, "mx", "my"),
            P("freq", None, None, "mx", "my"),
            P("mx", "my"),
            P("mx", "my"),
            P("mx", "my"),
            P("freq"),
            P(("mx", "my"), None),
            P(("mx", "my"), None),
            P(("mx", "my"), None),
        ),
        out_specs=(P("freq", None, None, "mx", "my"), P("mx", "my")),
        check_vma=False,
    )
```

profile of v0, /device:TPU:98, one launch (start us, length us, event | category | flops | bytes accessed | tf_op | source)
XLA Modules:
  0.0 1374.9 jit_solution(1580240488645792618)
XLA Ops:
  13.7 11.6 scatter_custom_fusion.1
  41.8 1255.3 %while.10 = (s32[]{:T(128)}, f32[6,64,256]{2,1,0:T(8,128)S(1)}, f32[64,256]{1,0:T(8,128)S(1)}, f32[6,64,256]{2,1,0:T(8,128)}, s32[2048]{0:T(1024)}, /*index=5*/s...) while((s32[]{:T(128)}, f32[6,64,256]{2,1,0:T(8,128)S(1)}, ...), condition=%wide.region_3.0_spmd, body=%wide.region_1.0_spmd.sunk | while | flops 2109442 | bytes 9095261 | solution.py:56
  56.7 11.4 all-to-all-start
  83.9 15.2 %scatter_custom_fusion.7 = f32[6,16384]{0,1:T(8,128)} fusion(s32[2048]{0:T(1024)S(1)} %bitcast.65, f32[2048,6]{1,0:T(8,128)S(1)} %copy.34, f32[]{:T(128)} %constant.21.clone.1..sunk), kind=kCustom, calls=%fused_computation.3.clone.1 | custom fusion | flops 12288 | bytes 393220 | tf_op jit(solution)/shard_map/while/body/eval_jaxpr/scatter-add | solution.py:43
  119.9 10.9 all-to-all-start
  146.7 15.2 %scatter_custom_fusion.7 = f32[6,16384]{0,1:T(8,128)} fusion(s32[2048]{0:T(1024)S(1)} %bitcast.65, f32[2048,6]{1,0:T(8,128)S(1)} %copy.34, f32[]{:T(128)} %constant.21.clone.1..sunk), kind=kCustom, calls=%fused_computation.3.clone.1 | custom fusion | flops 12288 | bytes 393220 | tf_op jit(solution)/shard_map/while/body/eval_jaxpr/scatter-add | solution.py:43
  182.6 10.9 all-to-all-start
  209.4 15.2 %scatter_custom_fusion.7 = f32[6,16384]{0,1:T(8,128)} fusion(s32[2048]{0:T(1024)S(1)} %bitcast.65, f32[2048,6]{1,0:T(8,128)S(1)} %copy.34, f32[]{:T(128)} %constant.21.clone.1..sunk), kind=kCustom, calls=%fused_computation.3.clone.1 | custom fusion | flops 12288 | bytes 393220 | tf_op jit(solution)/shard_map/while/body/eval_jaxpr/scatter-add | solution.py:43
  245.4 10.9 all-to-all-start
  272.1 15.2 %scatter_custom_fusion.7 = f32[6,16384]{0,1:T(8,128)} fusion(s32[2048]{0:T(1024)S(1)} %bitcast.65, f32[2048,6]{1,0:T(8,128)S(1)} %copy.34, f32[]{:T(128)} %constant.21.clone.1..sunk), kind=kCustom, calls=%fused_computation.3.clone.1 | custom fusion | flops 12288 | bytes 393220 | tf_op jit(solution)/shard_map/while/body/eval_jaxpr/scatter-add | solution.py:43
  308.1 10.9 all-to-all-start
  334.9 15.2 %scatter_custom_fusion.7 = f32[6,16384]{0,1:T(8,128)} fusion(s32[2048]{0:T(1024)S(1)} %bitcast.65, f32[2048,6]{1,0:T(8,128)S(1)} %copy.34, f32[]{:T(128)} %constant.21.clone.1..sunk), kind=kCustom, calls=%fused_computation.3.clone.1 | custom fusion | flops 12288 | bytes 393220 | tf_op jit(solution)/shard_map/while/body/eval_jaxpr/scatter-add | solution.py:43
  370.8 10.9 all-to-all-start
  397.6 15.2 %scatter_custom_fusion.7 = f32[6,16384]{0,1:T(8,128)} fusion(s32[2048]{0:T(1024)S(1)} %bitcast.65, f32[2048,6]{1,0:T(8,128)S(1)} %copy.34, f32[]{:T(128)} %constant.21.clone.1..sunk), kind=kCustom, calls=%fused_computation.3.clone.1 | custom fusion | flops 12288 | bytes 393220 | tf_op jit(solution)/shard_map/while/body/eval_jaxpr/scatter-add | solution.py:43
  433.6 10.9 all-to-all-start
  460.4 15.2 %scatter_custom_fusion.7 = f32[6,16384]{0,1:T(8,128)} fusion(s32[2048]{0:T(1024)S(1)} %bitcast.65, f32[2048,6]{1,0:T(8,128)S(1)} %copy.34, f32[]{:T(128)} %constant.21.clone.1..sunk), kind=kCustom, calls=%fused_computation.3.clone.1 | custom fusion | flops 12288 | bytes 393220 | tf_op jit(solution)/shard_map/while/body/eval_jaxpr/scatter-add | solution.py:43
  496.3 10.9 all-to-all-start
  523.1 15.2 %scatter_custom_fusion.7 = f32[6,16384]{0,1:T(8,128)} fusion(s32[2048]{0:T(1024)S(1)} %bitcast.65, f32[2048,6]{1,0:T(8,128)S(1)} %copy.34, f32[]{:T(128)} %constant.21.clone.1..sunk), kind=kCustom, calls=%fused_computation.3.clone.1 | custom fusion | flops 12288 | bytes 393220 | tf_op jit(solution)/shard_map/while/body/eval_jaxpr/scatter-add | solution.py:43
  559.1 10.9 all-to-all-start
  585.8 15.2 %scatter_custom_fusion.7 = f32[6,16384]{0,1:T(8,128)} fusion(s32[2048]{0:T(1024)S(1)} %bitcast.65, f32[2048,6]{1,0:T(8,128)S(1)} %copy.34, f32[]{:T(128)} %constant.21.clone.1..sunk), kind=kCustom, calls=%fused_computation.3.clone.1 | custom fusion | flops 12288 | bytes 393220 | tf_op jit(solution)/shard_map/while/body/eval_jaxpr/scatter-add | solution.py:43
  648.6 15.2 %scatter_custom_fusion.7 = f32[6,16384]{0,1:T(8,128)} fusion(s32[2048]{0:T(1024)S(1)} %bitcast.65, f32[2048,6]{1,0:T(8,128)S(1)} %copy.34, f32[]{:T(128)} %constant.21.clone.1..sunk), kind=kCustom, calls=%fused_computation.3.clone.1 | custom fusion | flops 12288 | bytes 393220 | tf_op jit(solution)/shard_map/while/body/eval_jaxpr/scatter-add | solution.py:43
  711.3 15.2 %scatter_custom_fusion.7 = f32[6,16384]{0,1:T(8,128)} fusion(s32[2048]{0:T(1024)S(1)} %bitcast.65, f32[2048,6]{1,0:T(8,128)S(1)} %copy.34, f32[]{:T(128)} %constant.21.clone.1..sunk), kind=kCustom, calls=%fused_computation.3.clone.1 | custom fusion | flops 12288 | bytes 393220 | tf_op jit(solution)/shard_map/while/body/eval_jaxpr/scatter-add | solution.py:43
  774.1 15.2 %scatter_custom_fusion.7 = f32[6,16384]{0,1:T(8,128)} fusion(s32[2048]{0:T(1024)S(1)} %bitcast.65, f32[2048,6]{1,0:T(8,128)S(1)} %copy.34, f32[]{:T(128)} %constant.21.clone.1..sunk), kind=kCustom, calls=%fused_computation.3.clone.1 | custom fusion | flops 12288 | bytes 393220 | tf_op jit(solution)/shard_map/while/body/eval_jaxpr/scatter-add | solution.py:43
  836.8 15.2 %scatter_custom_fusion.7 = f32[6,16384]{0,1:T(8,128)} fusion(s32[2048]{0:T(1024)S(1)} %bitcast.65, f32[2048,6]{1,0:T(8,128)S(1)} %copy.34, f32[]{:T(128)} %constant.21.clone.1..sunk), kind=kCustom, calls=%fused_computation.3.clone.1 | custom fusion | flops 12288 | bytes 393220 | tf_op jit(solution)/shard_map/while/body/eval_jaxpr/scatter-add | solution.py:43
  899.5 15.2 %scatter_custom_fusion.7 = f32[6,16384]{0,1:T(8,128)} fusion(s32[2048]{0:T(1024)S(1)} %bitcast.65, f32[2048,6]{1,0:T(8,128)S(1)} %copy.34, f32[]{:T(128)} %constant.21.clone.1..sunk), kind=kCustom, calls=%fused_computation.3.clone.1 | custom fusion | flops 12288 | bytes 393220 | tf_op jit(solution)/shard_map/while/body/eval_jaxpr/scatter-add | solution.py:43
  962.3 15.2 %scatter_custom_fusion.7 = f32[6,16384]{0,1:T(8,128)} fusion(s32[2048]{0:T(1024)S(1)} %bitcast.65, f32[2048,6]{1,0:T(8,128)S(1)} %copy.34, f32[]{:T(128)} %constant.21.clone.1..sunk), kind=kCustom, calls=%fused_computation.3.clone.1 | custom fusion | flops 12288 | bytes 393220 | tf_op jit(solution)/shard_map/while/body/eval_jaxpr/scatter-add | solution.py:43
  1025.0 15.2 %scatter_custom_fusion.7 = f32[6,16384]{0,1:T(8,128)} fusion(s32[2048]{0:T(1024)S(1)} %bitcast.65, f32[2048,6]{1,0:T(8,128)S(1)} %copy.34, f32[]{:T(128)} %constant.21.clone.1..sunk), kind=kCustom, calls=%fused_computation.3.clone.1 | custom fusion | flops 12288 | bytes 393220 | tf_op jit(solution)/shard_map/while/body/eval_jaxpr/scatter-add | solution.py:43
  1087.8 15.2 %scatter_custom_fusion.7 = f32[6,16384]{0,1:T(8,128)} fusion(s32[2048]{0:T(1024)S(1)} %bitcast.65, f32[2048,6]{1,0:T(8,128)S(1)} %copy.34, f32[]{:T(128)} %constant.21.clone.1..sunk), kind=kCustom, calls=%fused_computation.3.clone.1 | custom fusion | flops 12288 | bytes 393220 | tf_op jit(solution)/shard_map/while/body/eval_jaxpr/scatter-add | solution.py:43
  1150.5 15.2 %scatter_custom_fusion.7 = f32[6,16384]{0,1:T(8,128)} fusion(s32[2048]{0:T(1024)S(1)} %bitcast.65, f32[2048,6]{1,0:T(8,128)S(1)} %copy.34, f32[]{:T(128)} %constant.21.clone.1..sunk), kind=kCustom, calls=%fused_computation.3.clone.1 | custom fusion | flops 12288 | bytes 393220 | tf_op jit(solution)/shard_map/while/body/eval_jaxpr/scatter-add | solution.py:43
  1213.2 15.2 %scatter_custom_fusion.7 = f32[6,16384]{0,1:T(8,128)} fusion(s32[2048]{0:T(1024)S(1)} %bitcast.65, f32[2048,6]{1,0:T(8,128)S(1)} %copy.34, f32[]{:T(128)} %constant.21.clone.1..sunk), kind=kCustom, calls=%fused_computation.3.clone.1 | custom fusion | flops 12288 | bytes 393220 | tf_op jit(solution)/shard_map/while/body/eval_jaxpr/scatter-add | solution.py:43
  1276.0 15.2 %scatter_custom_fusion.7 = f32[6,16384]{0,1:T(8,128)} fusion(s32[2048]{0:T(1024)S(1)} %bitcast.65, f32[2048,6]{1,0:T(8,128)S(1)} %copy.34, f32[]{:T(128)} %constant.21.clone.1..sunk), kind=kCustom, calls=%fused_computation.3.clone.1 | custom fusion | flops 12288 | bytes 393220 | tf_op jit(solution)/shard_map/while/body/eval_jaxpr/scatter-add | solution.py:43
  1299.1 48.6 %all-reduce.2.cloned.1.call-done = f32[64,256]{1,0:T(8,128)} async-done(((f32[64,256]{1,0:T(8,128)}), f32[64,256]{1,0:T(8,128)}) %all-reduce.2.cloned.1.call-update) | async-done | bytes 65552 | tf_op jit(solution)/shard_map/psum | solution.py:71
  (814 shorter events, 891.6 us)
Async XLA Ops:
  7.2 1340.5 %all-reduce.2.cloned.1.call-start = ((), (), s32[]{:S(2)}) async-start(), calls=%async_computation.1 | async-start | bytes 131072 | tf_op jit(solution)/shard_map/psum | solution.py:71
  56.7 25.2 %all-to-all-start = ((f32[64,1,192]{2,1,0:T(1,128)}), f32[64,1,192]{2,1,0:T(1,128)S(1)}, u32[]{:S(2)}, u32[]{:S(2)}) async-start(f32[64,1,192]{2,1,0:T(1,128)} %reshape.136), calls=%async_computation | async-start | bytes 131072 | tf_op jit(solution)/shard_map/while/body/eval_jaxpr/all_to_all | solution.py:42
  75.4 29.1 %collective-permute-start.2 = (f32[6,66,1]{2,1,0:T(8,128)S(1)}, f32[6,66,1]{2,1,0:T(8,128)S(1)}, u32[]{:S(2)}, u32[]{:S(2)}) collective-permute-start(f32[6,66,1]{2,1,0:T(8,128)S(1)} %get-tuple-element.180), channel_id=1, source_target_pairs={{0,1},{1,2},{2,3},{3,4},{4,5},{5,6},{6,7},{8,9},{9,10},{10,11},{11... | collective-permute-start | bytes 4760 | tf_op jit(solution)/shard_map/while/body/eval_jaxpr/ppermute | solution.py:16
  119.9 24.8 %all-to-all-start = ((f32[64,1,192]{2,1,0:T(1,128)}), f32[64,1,192]{2,1,0:T(1,128)S(1)}, u32[]{:S(2)}, u32[]{:S(2)}) async-start(f32[64,1,192]{2,1,0:T(1,128)} %reshape.136), calls=%async_computation | async-start | bytes 131072 | tf_op jit(solution)/shard_map/while/body/eval_jaxpr/all_to_all | solution.py:42
  138.1 29.1 %collective-permute-start.2 = (f32[6,66,1]{2,1,0:T(8,128)S(1)}, f32[6,66,1]{2,1,0:T(8,128)S(1)}, u32[]{:S(2)}, u32[]{:S(2)}) collective-permute-start(f32[6,66,1]{2,1,0:T(8,128)S(1)} %get-tuple-element.180), channel_id=1, source_target_pairs={{0,1},{1,2},{2,3},{3,4},{4,5},{5,6},{6,7},{8,9},{9,10},{10,11},{11... | collective-permute-start | bytes 4760 | tf_op jit(solution)/shard_map/while/body/eval_jaxpr/ppermute | solution.py:16
  182.6 24.8 %all-to-all-start = ((f32[64,1,192]{2,1,0:T(1,128)}), f32[64,1,192]{2,1,0:T(1,128)S(1)}, u32[]{:S(2)}, u32[]{:S(2)}) async-start(f32[64,1,192]{2,1,0:T(1,128)} %reshape.136), calls=%async_computation | async-start | bytes 131072 | tf_op jit(solution)/shard_map/while/body/eval_jaxpr/all_to_all | solution.py:42
  200.9 29.1 %collective-permute-start.2 = (f32[6,66,1]{2,1,0:T(8,128)S(1)}, f32[6,66,1]{2,1,0:T(8,128)S(1)}, u32[]{:S(2)}, u32[]{:S(2)}) collective-permute-start(f32[6,66,1]{2,1,0:T(8,128)S(1)} %get-tuple-element.180), channel_id=1, source_target_pairs={{0,1},{1,2},{2,3},{3,4},{4,5},{5,6},{6,7},{8,9},{9,10},{10,11},{11... | collective-permute-start | bytes 4760 | tf_op jit(solution)/shard_map/while/body/eval_jaxpr/ppermute | solution.py:16
  245.4 24.8 %all-to-all-start = ((f32[64,1,192]{2,1,0:T(1,128)}), f32[64,1,192]{2,1,0:T(1,128)S(1)}, u32[]{:S(2)}, u32[]{:S(2)}) async-start(f32[64,1,192]{2,1,0:T(1,128)} %reshape.136), calls=%async_computation | async-start | bytes 131072 | tf_op jit(solution)/shard_map/while/body/eval_jaxpr/all_to_all | solution.py:42
  263.6 29.1 %collective-permute-start.2 = (f32[6,66,1]{2,1,0:T(8,128)S(1)}, f32[6,66,1]{2,1,0:T(8,128)S(1)}, u32[]{:S(2)}, u32[]{:S(2)}) collective-permute-start(f32[6,66,1]{2,1,0:T(8,128)S(1)} %get-tuple-element.180), channel_id=1, source_target_pairs={{0,1},{1,2},{2,3},{3,4},{4,5},{5,6},{6,7},{8,9},{9,10},{10,11},{11... | collective-permute-start | bytes 4760 | tf_op jit(solution)/shard_map/while/body/eval_jaxpr/ppermute | solution.py:16
  308.1 24.8 %all-to-all-start = ((f32[64,1,192]{2,1,0:T(1,128)}), f32[64,1,192]{2,1,0:T(1,128)S(1)}, u32[]{:S(2)}, u32[]{:S(2)}) async-start(f32[64,1,192]{2,1,0:T(1,128)} %reshape.136), calls=%async_computation | async-start | bytes 131072 | tf_op jit(solution)/shard_map/while/body/eval_jaxpr/all_to_all | solution.py:42
  326.4 29.1 %collective-permute-start.2 = (f32[6,66,1]{2,1,0:T(8,128)S(1)}, f32[6,66,1]{2,1,0:T(8,128)S(1)}, u32[]{:S(2)}, u32[]{:S(2)}) collective-permute-start(f32[6,66,1]{2,1,0:T(8,128)S(1)} %get-tuple-element.180), channel_id=1, source_target_pairs={{0,1},{1,2},{2,3},{3,4},{4,5},{5,6},{6,7},{8,9},{9,10},{10,11},{11... | collective-permute-start | bytes 4760 | tf_op jit(solution)/shard_map/while/body/eval_jaxpr/ppermute | solution.py:16
  370.8 24.8 %all-to-all-start = ((f32[64,1,192]{2,1,0:T(1,128)}), f32[64,1,192]{2,1,0:T(1,128)S(1)}, u32[]{:S(2)}, u32[]{:S(2)}) async-start(f32[64,1,192]{2,1,0:T(1,128)} %reshape.136), calls=%async_computation | async-start | bytes 131072 | tf_op jit(solution)/shard_map/while/body/eval_jaxpr/all_to_all | solution.py:42
  389.1 29.1 %collective-permute-start.2 = (f32[6,66,1]{2,1,0:T(8,128)S(1)}, f32[6,66,1]{2,1,0:T(8,128)S(1)}, u32[]{:S(2)}, u32[]{:S(2)}) collective-permute-start(f32[6,66,1]{2,1,0:T(8,128)S(1)} %get-tuple-element.180), channel_id=1, source_target_pairs={{0,1},{1,2},{2,3},{3,4},{4,5},{5,6},{6,7},{8,9},{9,10},{10,11},{11... | collective-permute-start | bytes 4760 | tf_op jit(solution)/shard_map/while/body/eval_jaxpr/ppermute | solution.py:16
  433.6 24.8 %all-to-all-start = ((f32[64,1,192]{2,1,0:T(1,128)}), f32[64,1,192]{2,1,0:T(1,128)S(1)}, u32[]{:S(2)}, u32[]{:S(2)}) async-start(f32[64,1,192]{2,1,0:T(1,128)} %reshape.136), calls=%async_computation | async-start | bytes 131072 | tf_op jit(solution)/shard_map/while/body/eval_jaxpr/all_to_all | solution.py:42
  451.8 29.1 %collective-permute-start.2 = (f32[6,66,1]{2,1,0:T(8,128)S(1)}, f32[6,66,1]{2,1,0:T(8,128)S(1)}, u32[]{:S(2)}, u32[]{:S(2)}) collective-permute-start(f32[6,66,1]{2,1,0:T(8,128)S(1)} %get-tuple-element.180), channel_id=1, source_target_pairs={{0,1},{1,2},{2,3},{3,4},{4,5},{5,6},{6,7},{8,9},{9,10},{10,11},{11... | collective-permute-start | bytes 4760 | tf_op jit(solution)/shard_map/while/body/eval_jaxpr/ppermute | solution.py:16
  496.3 24.8 %all-to-all-start = ((f32[64,1,192]{2,1,0:T(1,128)}), f32[64,1,192]{2,1,0:T(1,128)S(1)}, u32[]{:S(2)}, u32[]{:S(2)}) async-start(f32[64,1,192]{2,1,0:T(1,128)} %reshape.136), calls=%async_computation | async-start | bytes 131072 | tf_op jit(solution)/shard_map/while/body/eval_jaxpr/all_to_all | solution.py:42
  514.6 29.1 %collective-permute-start.2 = (f32[6,66,1]{2,1,0:T(8,128)S(1)}, f32[6,66,1]{2,1,0:T(8,128)S(1)}, u32[]{:S(2)}, u32[]{:S(2)}) collective-permute-start(f32[6,66,1]{2,1,0:T(8,128)S(1)} %get-tuple-element.180), channel_id=1, source_target_pairs={{0,1},{1,2},{2,3},{3,4},{4,5},{5,6},{6,7},{8,9},{9,10},{10,11},{11... | collective-permute-start | bytes 4760 | tf_op jit(solution)/shard_map/while/body/eval_jaxpr/ppermute | solution.py:16
  559.1 24.8 %all-to-all-start = ((f32[64,1,192]{2,1,0:T(1,128)}), f32[64,1,192]{2,1,0:T(1,128)S(1)}, u32[]{:S(2)}, u32[]{:S(2)}) async-start(f32[64,1,192]{2,1,0:T(1,128)} %reshape.136), calls=%async_computation | async-start | bytes 131072 | tf_op jit(solution)/shard_map/while/body/eval_jaxpr/all_to_all | solution.py:42
  577.3 29.1 %collective-permute-start.2 = (f32[6,66,1]{2,1,0:T(8,128)S(1)}, f32[6,66,1]{2,1,0:T(8,128)S(1)}, u32[]{:S(2)}, u32[]{:S(2)}) collective-permute-start(f32[6,66,1]{2,1,0:T(8,128)S(1)} %get-tuple-element.180), channel_id=1, source_target_pairs={{0,1},{1,2},{2,3},{3,4},{4,5},{5,6},{6,7},{8,9},{9,10},{10,11},{11... | collective-permute-start | bytes 4760 | tf_op jit(solution)/shard_map/while/body/eval_jaxpr/ppermute | solution.py:16
  621.8 24.8 %all-to-all-start = ((f32[64,1,192]{2,1,0:T(1,128)}), f32[64,1,192]{2,1,0:T(1,128)S(1)}, u32[]{:S(2)}, u32[]{:S(2)}) async-start(f32[64,1,192]{2,1,0:T(1,128)} %reshape.136), calls=%async_computation | async-start | bytes 131072 | tf_op jit(solution)/shard_map/while/body/eval_jaxpr/all_to_all | solution.py:42
  640.1 29.1 %collective-permute-start.2 = (f32[6,66,1]{2,1,0:T(8,128)S(1)}, f32[6,66,1]{2,1,0:T(8,128)S(1)}, u32[]{:S(2)}, u32[]{:S(2)}) collective-permute-start(f32[6,66,1]{2,1,0:T(8,128)S(1)} %get-tuple-element.180), channel_id=1, source_target_pairs={{0,1},{1,2},{2,3},{3,4},{4,5},{5,6},{6,7},{8,9},{9,10},{10,11},{11... | collective-permute-start | bytes 4760 | tf_op jit(solution)/shard_map/while/body/eval_jaxpr/ppermute | solution.py:16
  684.5 24.8 %all-to-all-start = ((f32[64,1,192]{2,1,0:T(1,128)}), f32[64,1,192]{2,1,0:T(1,128)S(1)}, u32[]{:S(2)}, u32[]{:S(2)}) async-start(f32[64,1,192]{2,1,0:T(1,128)} %reshape.136), calls=%async_computation | async-start | bytes 131072 | tf_op jit(solution)/shard_map/while/body/eval_jaxpr/all_to_all | solution.py:42
  702.8 29.1 %collective-permute-start.2 = (f32[6,66,1]{2,1,0:T(8,128)S(1)}, f32[6,66,1]{2,1,0:T(8,128)S(1)}, u32[]{:S(2)}, u32[]{:S(2)}) collective-permute-start(f32[6,66,1]{2,1,0:T(8,128)S(1)} %get-tuple-element.180), channel_id=1, source_target_pairs={{0,1},{1,2},{2,3},{3,4},{4,5},{5,6},{6,7},{8,9},{9,10},{10,11},{11... | collective-permute-start | bytes 4760 | tf_op jit(solution)/shard_map/while/body/eval_jaxpr/ppermute | solution.py:16
  765.5 29.1 %collective-permute-start.2 = (f32[6,66,1]{2,1,0:T(8,128)S(1)}, f32[6,66,1]{2,1,0:T(8,128)S(1)}, u32[]{:S(2)}, u32[]{:S(2)}) collective-permute-start(f32[6,66,1]{2,1,0:T(8,128)S(1)} %get-tuple-element.180), channel_id=1, source_target_pairs={{0,1},{1,2},{2,3},{3,4},{4,5},{5,6},{6,7},{8,9},{9,10},{10,11},{11... | collective-permute-start | bytes 4760 | tf_op jit(solution)/shard_map/while/body/eval_jaxpr/ppermute | solution.py:16
  828.3 29.1 %collective-permute-start.2 = (f32[6,66,1]{2,1,0:T(8,128)S(1)}, f32[6,66,1]{2,1,0:T(8,128)S(1)}, u32[]{:S(2)}, u32[]{:S(2)}) collective-permute-start(f32[6,66,1]{2,1,0:T(8,128)S(1)} %get-tuple-element.180), channel_id=1, source_target_pairs={{0,1},{1,2},{2,3},{3,4},{4,5},{5,6},{6,7},{8,9},{9,10},{10,11},{11... | collective-permute-start | bytes 4760 | tf_op jit(solution)/shard_map/while/body/eval_jaxpr/ppermute | solution.py:16
  891.0 29.1 %collective-permute-start.2 = (f32[6,66,1]{2,1,0:T(8,128)S(1)}, f32[6,66,1]{2,1,0:T(8,128)S(1)}, u32[]{:S(2)}, u32[]{:S(2)}) collective-permute-start(f32[6,66,1]{2,1,0:T(8,128)S(1)} %get-tuple-element.180), channel_id=1, source_target_pairs={{0,1},{1,2},{2,3},{3,4},{4,5},{5,6},{6,7},{8,9},{9,10},{10,11},{11... | collective-permute-start | bytes 4760 | tf_op jit(solution)/shard_map/while/body/eval_jaxpr/ppermute | solution.py:16
  953.8 29.1 %collective-permute-start.2 = (f32[6,66,1]{2,1,0:T(8,128)S(1)}, f32[6,66,1]{2,1,0:T(8,128)S(1)}, u32[]{:S(2)}, u32[]{:S(2)}) collective-permute-start(f32[6,66,1]{2,1,0:T(8,128)S(1)} %get-tuple-element.180), channel_id=1, source_target_pairs={{0,1},{1,2},{2,3},{3,4},{4,5},{5,6},{6,7},{8,9},{9,10},{10,11},{11... | collective-permute-start | bytes 4760 | tf_op jit(solution)/shard_map/while/body/eval_jaxpr/ppermute | solution.py:16
  1016.5 29.1 %collective-permute-start.2 = (f32[6,66,1]{2,1,0:T(8,128)S(1)}, f32[6,66,1]{2,1,0:T(8,128)S(1)}, u32[]{:S(2)}, u32[]{:S(2)}) collective-permute-start(f32[6,66,1]{2,1,0:T(8,128)S(1)} %get-tuple-element.180), channel_id=1, source_target_pairs={{0,1},{1,2},{2,3},{3,4},{4,5},{5,6},{6,7},{8,9},{9,10},{10,11},{11... | collective-permute-start | bytes 4760 | tf_op jit(solution)/shard_map/while/body/eval_jaxpr/ppermute | solution.py:16
  1079.2 29.1 %collective-permute-start.2 = (f32[6,66,1]{2,1,0:T(8,128)S(1)}, f32[6,66,1]{2,1,0:T(8,128)S(1)}, u32[]{:S(2)}, u32[]{:S(2)}) collective-permute-start(f32[6,66,1]{2,1,0:T(8,128)S(1)} %get-tuple-element.180), channel_id=1, source_target_pairs={{0,1},{1,2},{2,3},{3,4},{4,5},{5,6},{6,7},{8,9},{9,10},{10,11},{11... | collective-permute-start | bytes 4760 | tf_op jit(solution)/shard_map/while/body/eval_jaxpr/ppermute | solution.py:16
  1142.0 29.1 %collective-permute-start.2 = (f32[6,66,1]{2,1,0:T(8,128)S(1)}, f32[6,66,1]{2,1,0:T(8,128)S(1)}, u32[]{:S(2)}, u32[]{:S(2)}) collective-permute-start(f32[6,66,1]{2,1,0:T(8,128)S(1)} %get-tuple-element.180), channel_id=1, source_target_pairs={{0,1},{1,2},{2,3},{3,4},{4,5},{5,6},{6,7},{8,9},{9,10},{10,11},{11... | collective-permute-start | bytes 4760 | tf_op jit(solution)/shard_map/while/body/eval_jaxpr/ppermute | solution.py:16
  1204.7 29.1 %collective-permute-start.2 = (f32[6,66,1]{2,1,0:T(8,128)S(1)}, f32[6,66,1]{2,1,0:T(8,128)S(1)}, u32[]{:S(2)}, u32[]{:S(2)}) collective-permute-start(f32[6,66,1]{2,1,0:T(8,128)S(1)} %get-tuple-element.180), channel_id=1, source_target_pairs={{0,1},{1,2},{2,3},{3,4},{4,5},{5,6},{6,7},{8,9},{9,10},{10,11},{11... | collective-permute-start | bytes 4760 | tf_op jit(solution)/shard_map/while/body/eval_jaxpr/ppermute | solution.py:16
  1267.5 29.1 %collective-permute-start.2 = (f32[6,66,1]{2,1,0:T(8,128)S(1)}, f32[6,66,1]{2,1,0:T(8,128)S(1)}, u32[]{:S(2)}, u32[]{:S(2)}) collective-permute-start(f32[6,66,1]{2,1,0:T(8,128)S(1)} %get-tuple-element.180), channel_id=1, source_target_pairs={{0,1},{1,2},{2,3},{3,4},{4,5},{5,6},{6,7},{8,9},{9,10},{10,11},{11... | collective-permute-start | bytes 4760 | tf_op jit(solution)/shard_map/while/body/eval_jaxpr/ppermute | solution.py:16
  (160 other events, 4304.2 us)
Sparse Core Ops, SparseCore 0:
  1299.2 48.4 all-reduce.1
where the time goes:
time: 1380 us; the launch traced here: 1370 us
  starting transfers between devices  458 us (33%)
  local copies, waits for them, and re-layouts  429 us (31%)
  other arithmetic  355 us (26%)
  waiting for transfers between devices  113 us (8%)
  between operations  14.9 us (1%)
    scatter-add x20, other arithmetic, mortar(): added = jnp.zeros((6, cells), jnp.float32).at[:, targets].add(got * weights)  304 us
    all_to_all x20, starting transfers between devices, mortar(): lax.all_to_all(sent, ('mx', 'my'), split_axis=1, concat_axis=1, tiled=True)  219 us
    gather x20, local copies, waits for them, and re-layouts, mortar(): sent = field.reshape(6, cells)[:, sources]  177 us
    ppermute x44, starting transfers between devices, extended(): before = lax.ppermute(last, axis, up)  149 us
    reshape x20, local copies, waits for them, and re-layouts, mortar(): return added.reshape(6, rows_x, rows_y)  106 us
    another operation x20, local copies, waits for them, and re-layouts  94.6 us
    ppermute x44, starting transfers between devices, extended(): after = lax.ppermute(first, axis, down)  89.9 us
    ppermute x44, waiting for transfers between devices, extended(): before = lax.ppermute(last, axis, up)  59.5 us
  transfers between devices with their start and end apart: 109, of which 25 were waited for; matrix products, arithmetic and copies ran while one was open for 34% of the time, Pallas kernels for 0%

commit v1 on v0

--- a/solution.py
+++ b/solution.py
@@ -68,7 +68,7 @@
     t_re = da * u[:3] - db * u[3:] - dstiff * nb[:3]
     t_im = da * u[3:] + db * u[:3] - dstiff * nb[3:]
     sens = -jnp.sum(field[:3] * t_re - field[3:] * t_im, axis=0)
-    total = lax.psum(sens, "freq")
+    total = jnp.sum(lax.all_gather(sens, "freq"), axis=0)
     weighted = extended(density * total, (("mx", 0), ("my", 1)), 1)
     filt = weighted[1:-1, 1:-1]
     filt = filt + 0.5 * (

time: 1380 us -> 1330 us (0.964)
  waiting for transfers between devices: 113 us -> 64.8 us
    psum x1 -> x0, waiting for transfers between devices: 48.6 us -> none  [on_device(): total = lax.psum(sens, 'freq')]
  transfers between devices with their start and end apart: 109 -> 108, of which waited for: 25 -> 24; matrix products, arithmetic and copies ran while one was open for 34% -> 35% of each run, Pallas kernels for 0% -> 0%
where the time goes in v1:
time: 1330 us; the launch traced here: 1320 us
  starting transfers between devices  458 us (34%)
  local copies, waits for them, and re-layouts  429 us (32%)
  other arithmetic  353 us (27%)
  waiting for transfers between devices  64.8 us (5%)
    scatter-add x20, other arithmetic, mortar(): added = jnp.zeros((6, cells), jnp.float32).at[:, targets].add(got * weights)  304 us
    all_to_all x20, starting transfers between devices, mortar(): lax.all_to_all(sent, ('mx', 'my'), split_axis=1, concat_axis=1, tiled=True)  219 us
    gather x20, local copies, waits for them, and re-layouts, mortar(): sent = field.reshape(6, cells)[:, sources]  177 us
    ppermute x44, starting transfers between devices, extended(): before = lax.ppermute(last, axis, up)  150 us
    reshape x20, local copies, waits for them, and re-layouts, mortar(): return added.reshape(6, rows_x, rows_y)  106 us
    another operation x20, local copies, waits for them, and re-layouts  94.2 us
    ppermute x44, starting transfers between devices, extended(): after = lax.ppermute(first, axis, down)  89.9 us
    ppermute x44, waiting for transfers between devices, extended(): before = lax.ppermute(last, axis, up)  59.5 us
  transfers between devices with their start and end apart: 108, of which 24 were waited for; matrix products, arithmetic and copies ran while one was open for 35% of the time, Pallas kernels for 0%

profile of v1, /device:TPU:98, one launch (start us, length us, event | category | flops | bytes accessed | tf_op | source)
XLA Modules:
  0.0 1324.3 jit_solution(2179315133609839198)
XLA Ops:
  7.1 11.6 scatter_custom_fusion.1
  35.2 1254.8 %while.10 = (s32[]{:T(128)}, f32[6,64,256]{2,1,0:T(8,128)S(1)}, f32[64,256]{1,0:T(8,128)S(1)}, f32[6,64,256]{2,1,0:T(8,128)}, s32[2048]{0:T(1024)}, /*index=5*/s...) while((s32[]{:T(128)}, f32[6,64,256]{2,1,0:T(8,128)S(1)}, ...), condition=%wide.region_3.0_spmd, body=%wide.region_1.0_spmd.sunk | while | flops 2109442 | bytes 9095261 | solution.py:56
  50.1 11.4 all-to-all-start
  77.3 15.2 %scatter_custom_fusion.7 = f32[6,16384]{0,1:T(8,128)} fusion(s32[2048]{0:T(1024)S(1)} %bitcast.67, f32[2048,6]{1,0:T(8,128)S(1)} %copy.39, f32[]{:T(128)} %constant.21.clone.1..sunk), kind=kCustom, calls=%fused_computation.3.clone.1 | custom fusion | flops 12288 | bytes 393220 | tf_op jit(solution)/shard_map/while/body/eval_jaxpr/scatter-add | solution.py:43
  113.2 10.9 all-to-all-start
  140.0 15.2 %scatter_custom_fusion.7 = f32[6,16384]{0,1:T(8,128)} fusion(s32[2048]{0:T(1024)S(1)} %bitcast.67, f32[2048,6]{1,0:T(8,128)S(1)} %copy.39, f32[]{:T(128)} %constant.21.clone.1..sunk), kind=kCustom, calls=%fused_computation.3.clone.1 | custom fusion | flops 12288 | bytes 393220 | tf_op jit(solution)/shard_map/while/body/eval_jaxpr/scatter-add | solution.py:43
  176.0 10.9 all-to-all-start
  202.8 15.2 %scatter_custom_fusion.7 = f32[6,16384]{0,1:T(8,128)} fusion(s32[2048]{0:T(1024)S(1)} %bitcast.67, f32[2048,6]{1,0:T(8,128)S(1)} %copy.39, f32[]{:T(128)} %constant.21.clone.1..sunk), kind=kCustom, calls=%fused_computation.3.clone.1 | custom fusion | flops 12288 | bytes 393220 | tf_op jit(solution)/shard_map/while/body/eval_jaxpr/scatter-add | solution.py:43
  238.7 10.9 all-to-all-start
  265.5 15.2 %scatter_custom_fusion.7 = f32[6,16384]{0,1:T(8,128)} fusion(s32[2048]{0:T(1024)S(1)} %bitcast.67, f32[2048,6]{1,0:T(8,128)S(1)} %copy.39, f32[]{:T(128)} %constant.21.clone.1..sunk), kind=kCustom, calls=%fused_computation.3.clone.1 | custom fusion | flops 12288 | bytes 393220 | tf_op jit(solution)/shard_map/while/body/eval_jaxpr/scatter-add | solution.py:43
  301.4 10.9 all-to-all-start
  328.2 15.2 %scatter_custom_fusion.7 = f32[6,16384]{0,1:T(8,128)} fusion(s32[2048]{0:T(1024)S(1)} %bitcast.67, f32[2048,6]{1,0:T(8,128)S(1)} %copy.39, f32[]{:T(128)} %constant.21.clone.1..sunk), kind=kCustom, calls=%fused_computation.3.clone.1 | custom fusion | flops 12288 | bytes 393220 | tf_op jit(solution)/shard_map/while/body/eval_jaxpr/scatter-add | solution.py:43
  364.1 10.9 all-to-all-start
  390.9 15.2 %scatter_custom_fusion.7 = f32[6,16384]{0,1:T(8,128)} fusion(s32[2048]{0:T(1024)S(1)} %bitcast.67, f32[2048,6]{1,0:T(8,128)S(1)} %copy.39, f32[]{:T(128)} %constant.21.clone.1..sunk), kind=kCustom, calls=%fused_computation.3.clone.1 | custom fusion | flops 12288 | bytes 393220 | tf_op jit(solution)/shard_map/while/body/eval_jaxpr/scatter-add | solution.py:43
  426.8 10.9 all-to-all-start
  453.6 15.2 %scatter_custom_fusion.7 = f32[6,16384]{0,1:T(8,128)} fusion(s32[2048]{0:T(1024)S(1)} %bitcast.67, f32[2048,6]{1,0:T(8,128)S(1)} %copy.39, f32[]{:T(128)} %constant.21.clone.1..sunk), kind=kCustom, calls=%fused_computation.3.clone.1 | custom fusion | flops 12288 | bytes 393220 | tf_op jit(solution)/shard_map/while/body/eval_jaxpr/scatter-add | solution.py:43
  489.6 10.9 all-to-all-start
  516.3 15.2 %scatter_custom_fusion.7 = f32[6,16384]{0,1:T(8,128)} fusion(s32[2048]{0:T(1024)S(1)} %bitcast.67, f32[2048,6]{1,0:T(8,128)S(1)} %copy.39, f32[]{:T(128)} %constant.21.clone.1..sunk), kind=kCustom, calls=%fused_computation.3.clone.1 | custom fusion | flops 12288 | bytes 393220 | tf_op jit(solution)/shard_map/while/body/eval_jaxpr/scatter-add | solution.py:43
  552.3 10.9 all-to-all-start
  579.1 15.2 %scatter_custom_fusion.7 = f32[6,16384]{0,1:T(8,128)} fusion(s32[2048]{0:T(1024)S(1)} %bitcast.67, f32[2048,6]{1,0:T(8,128)S(1)} %copy.39, f32[]{:T(128)} %constant.21.clone.1..sunk), kind=kCustom, calls=%fused_computation.3.clone.1 | custom fusion | flops 12288 | bytes 393220 | tf_op jit(solution)/shard_map/while/body/eval_jaxpr/scatter-add | solution.py:43
  641.8 15.2 %scatter_custom_fusion.7 = f32[6,16384]{0,1:T(8,128)} fusion(s32[2048]{0:T(1024)S(1)} %bitcast.67, f32[2048,6]{1,0:T(8,128)S(1)} %copy.39, f32[]{:T(128)} %constant.21.clone.1..sunk), kind=kCustom, calls=%fused_computation.3.clone.1 | custom fusion | flops 12288 | bytes 393220 | tf_op jit(solution)/shard_map/while/body/eval_jaxpr/scatter-add | solution.py:43
  704.5 15.2 %scatter_custom_fusion.7 = f32[6,16384]{0,1:T(8,128)} fusion(s32[2048]{0:T(1024)S(1)} %bitcast.67, f32[2048,6]{1,0:T(8,128)S(1)} %copy.39, f32[]{:T(128)} %constant.21.clone.1..sunk), kind=kCustom, calls=%fused_computation.3.clone.1 | custom fusion | flops 12288 | bytes 393220 | tf_op jit(solution)/shard_map/while/body/eval_jaxpr/scatter-add | solution.py:43
  767.2 15.2 %scatter_custom_fusion.7 = f32[6,16384]{0,1:T(8,128)} fusion(s32[2048]{0:T(1024)S(1)} %bitcast.67, f32[2048,6]{1,0:T(8,128)S(1)} %copy.39, f32[]{:T(128)} %constant.21.clone.1..sunk), kind=kCustom, calls=%fused_computation.3.clone.1 | custom fusion | flops 12288 | bytes 393220 | tf_op jit(solution)/shard_map/while/body/eval_jaxpr/scatter-add | solution.py:43
  829.9 15.2 %scatter_custom_fusion.7 = f32[6,16384]{0,1:T(8,128)} fusion(s32[2048]{0:T(1024)S(1)} %bitcast.67, f32[2048,6]{1,0:T(8,128)S(1)} %copy.39, f32[]{:T(128)} %constant.21.clone.1..sunk), kind=kCustom, calls=%fused_computation.3.clone.1 | custom fusion | flops 12288 | bytes 393220 | tf_op jit(solution)/shard_map/while/body/eval_jaxpr/scatter-add | solution.py:43
  892.7 15.2 %scatter_custom_fusion.7 = f32[6,16384]{0,1:T(8,128)} fusion(s32[2048]{0:T(1024)S(1)} %bitcast.67, f32[2048,6]{1,0:T(8,128)S(1)} %copy.39, f32[]{:T(128)} %constant.21.clone.1..sunk), kind=kCustom, calls=%fused_computation.3.clone.1 | custom fusion | flops 12288 | bytes 393220 | tf_op jit(solution)/shard_map/while/body/eval_jaxpr/scatter-add | solution.py:43
  955.4 15.2 %scatter_custom_fusion.7 = f32[6,16384]{0,1:T(8,128)} fusion(s32[2048]{0:T(1024)S(1)} %bitcast.67, f32[2048,6]{1,0:T(8,128)S(1)} %copy.39, f32[]{:T(128)} %constant.21.clone.1..sunk), kind=kCustom, calls=%fused_computation.3.clone.1 | custom fusion | flops 12288 | bytes 393220 | tf_op jit(solution)/shard_map/while/body/eval_jaxpr/scatter-add | solution.py:43
  1018.1 15.2 %scatter_custom_fusion.7 = f32[6,16384]{0,1:T(8,128)} fusion(s32[2048]{0:T(1024)S(1)} %bitcast.67, f32[2048,6]{1,0:T(8,128)S(1)} %copy.39, f32[]{:T(128)} %constant.21.clone.1..sunk), kind=kCustom, calls=%fused_computation.3.clone.1 | custom fusion | flops 12288 | bytes 393220 | tf_op jit(solution)/shard_map/while/body/eval_jaxpr/scatter-add | solution.py:43
  1080.8 15.2 %scatter_custom_fusion.7 = f32[6,16384]{0,1:T(8,128)} fusion(s32[2048]{0:T(1024)S(1)} %bitcast.67, f32[2048,6]{1,0:T(8,128)S(1)} %copy.39, f32[]{:T(128)} %constant.21.clone.1..sunk), kind=kCustom, calls=%fused_computation.3.clone.1 | custom fusion | flops 12288 | bytes 393220 | tf_op jit(solution)/shard_map/while/body/eval_jaxpr/scatter-add | solution.py:43
  1143.5 15.2 %scatter_custom_fusion.7 = f32[6,16384]{0,1:T(8,128)} fusion(s32[2048]{0:T(1024)S(1)} %bitcast.67, f32[2048,6]{1,0:T(8,128)S(1)} %copy.39, f32[]{:T(128)} %constant.21.clone.1..sunk), kind=kCustom, calls=%fused_computation.3.clone.1 | custom fusion | flops 12288 | bytes 393220 | tf_op jit(solution)/shard_map/while/body/eval_jaxpr/scatter-add | solution.py:43
  1206.3 15.2 %scatter_custom_fusion.7 = f32[6,16384]{0,1:T(8,128)} fusion(s32[2048]{0:T(1024)S(1)} %bitcast.67, f32[2048,6]{1,0:T(8,128)S(1)} %copy.39, f32[]{:T(128)} %constant.21.clone.1..sunk), kind=kCustom, calls=%fused_computation.3.clone.1 | custom fusion | flops 12288 | bytes 393220 | tf_op jit(solution)/shard_map/while/body/eval_jaxpr/scatter-add | solution.py:43
  1269.0 15.2 %scatter_custom_fusion.7 = f32[6,16384]{0,1:T(8,128)} fusion(s32[2048]{0:T(1024)S(1)} %bitcast.67, f32[2048,6]{1,0:T(8,128)S(1)} %copy.39, f32[]{:T(128)} %constant.21.clone.1..sunk), kind=kCustom, calls=%fused_computation.3.clone.1 | custom fusion | flops 12288 | bytes 393220 | tf_op jit(solution)/shard_map/while/body/eval_jaxpr/scatter-add | solution.py:43
  1291.4 12.8 all-gather
  (813 shorter events, 890.3 us)
Async XLA Ops:
  50.1 25.2 %all-to-all-start = ((f32[64,1,192]{2,1,0:T(1,128)}), f32[64,1,192]{2,1,0:T(1,128)S(1)}, u32[]{:S(2)}, u32[]{:S(2)}) async-start(f32[64,1,192]{2,1,0:T(1,128)} %reshape.145), calls=%async_computation | async-start | bytes 131072 | tf_op jit(solution)/shard_map/while/body/eval_jaxpr/all_to_all | solution.py:42
  68.8 29.1 %collective-permute-start.2 = (f32[6,66,1]{2,1,0:T(8,128)S(1)}, f32[6,66,1]{2,1,0:T(8,128)S(1)}, u32[]{:S(2)}, u32[]{:S(2)}) collective-permute-start(f32[6,66,1]{2,1,0:T(8,128)S(1)} %get-tuple-element.180), channel_id=1, source_target_pairs={{0,1},{1,2},{2,3},{3,4},{4,5},{5,6},{6,7},{8,9},{9,10},{10,11},{11... | collective-permute-start | bytes 4760 | tf_op jit(solution)/shard_map/while/body/eval_jaxpr/ppermute | solution.py:16
  113.2 24.8 %all-to-all-start = ((f32[64,1,192]{2,1,0:T(1,128)}), f32[64,1,192]{2,1,0:T(1,128)S(1)}, u32[]{:S(2)}, u32[]{:S(2)}) async-start(f32[64,1,192]{2,1,0:T(1,128)} %reshape.145), calls=%async_computation | async-start | bytes 131072 | tf_op jit(solution)/shard_map/while/body/eval_jaxpr/all_to_all | solution.py:42
  131.5 29.1 %collective-permute-start.2 = (f32[6,66,1]{2,1,0:T(8,128)S(1)}, f32[6,66,1]{2,1,0:T(8,128)S(1)}, u32[]{:S(2)}, u32[]{:S(2)}) collective-permute-start(f32[6,66,1]{2,1,0:T(8,128)S(1)} %get-tuple-element.180), channel_id=1, source_target_pairs={{0,1},{1,2},{2,3},{3,4},{4,5},{5,6},{6,7},{8,9},{9,10},{10,11},{11... | collective-permute-start | bytes 4760 | tf_op jit(solution)/shard_map/while/body/eval_jaxpr/ppermute | solution.py:16
  176.0 24.8 %all-to-all-start = ((f32[64,1,192]{2,1,0:T(1,128)}), f32[64,1,192]{2,1,0:T(1,128)S(1)}, u32[]{:S(2)}, u32[]{:S(2)}) async-start(f32[64,1,192]{2,1,0:T(1,128)} %reshape.145), calls=%async_computation | async-start | bytes 131072 | tf_op jit(solution)/shard_map/while/body/eval_jaxpr/all_to_all | solution.py:42
  194.2 29.1 %collective-permute-start.2 = (f32[6,66,1]{2,1,0:T(8,128)S(1)}, f32[6,66,1]{2,1,0:T(8,128)S(1)}, u32[]{:S(2)}, u32[]{:S(2)}) collective-permute-start(f32[6,66,1]{2,1,0:T(8,128)S(1)} %get-tuple-element.180), channel_id=1, source_target_pairs={{0,1},{1,2},{2,3},{3,4},{4,5},{5,6},{6,7},{8,9},{9,10},{10,11},{11... | collective-permute-start | bytes 4760 | tf_op jit(solution)/shard_map/while/body/eval_jaxpr/ppermute | solution.py:16
  238.7 24.8 %all-to-all-start = ((f32[64,1,192]{2,1,0:T(1,128)}), f32[64,1,192]{2,1,0:T(1,128)S(1)}, u32[]{:S(2)}, u32[]{:S(2)}) async-start(f32[64,1,192]{2,1,0:T(1,128)} %reshape.145), calls=%async_computation | async-start | bytes 131072 | tf_op jit(solution)/shard_map/while/body/eval_jaxpr/all_to_all | solution.py:42
  256.9 29.1 %collective-permute-start.2 = (f32[6,66,1]{2,1,0:T(8,128)S(1)}, f32[6,66,1]{2,1,0:T(8,128)S(1)}, u32[]{:S(2)}, u32[]{:S(2)}) collective-permute-start(f32[6,66,1]{2,1,0:T(8,128)S(1)} %get-tuple-element.180), channel_id=1, source_target_pairs={{0,1},{1,2},{2,3},{3,4},{4,5},{5,6},{6,7},{8,9},{9,10},{10,11},{11... | collective-permute-start | bytes 4760 | tf_op jit(solution)/shard_map/while/body/eval_jaxpr/ppermute | solution.py:16
  301.4 24.8 %all-to-all-start = ((f32[64,1,192]{2,1,0:T(1,128)}), f32[64,1,192]{2,1,0:T(1,128)S(1)}, u32[]{:S(2)}, u32[]{:S(2)}) async-start(f32[64,1,192]{2,1,0:T(1,128)} %reshape.145), calls=%async_computation | async-start | bytes 131072 | tf_op jit(solution)/shard_map/while/body/eval_jaxpr/all_to_all | solution.py:42
  319.7 29.1 %collective-permute-start.2 = (f32[6,66,1]{2,1,0:T(8,128)S(1)}, f32[6,66,1]{2,1,0:T(8,128)S(1)}, u32[]{:S(2)}, u32[]{:S(2)}) collective-permute-start(f32[6,66,1]{2,1,0:T(8,128)S(1)} %get-tuple-element.180), channel_id=1, source_target_pairs={{0,1},{1,2},{2,3},{3,4},{4,5},{5,6},{6,7},{8,9},{9,10},{10,11},{11... | collective-permute-start | bytes 4760 | tf_op jit(solution)/shard_map/while/body/eval_jaxpr/ppermute | solution.py:16
  364.1 24.8 %all-to-all-start = ((f32[64,1,192]{2,1,0:T(1,128)}), f32[64,1,192]{2,1,0:T(1,128)S(1)}, u32[]{:S(2)}, u32[]{:S(2)}) async-start(f32[64,1,192]{2,1,0:T(1,128)} %reshape.145), calls=%async_computation | async-start | bytes 131072 | tf_op jit(solution)/shard_map/while/body/eval_jaxpr/all_to_all | solution.py:42
  382.4 29.1 %collective-permute-start.2 = (f32[6,66,1]{2,1,0:T(8,128)S(1)}, f32[6,66,1]{2,1,0:T(8,128)S(1)}, u32[]{:S(2)}, u32[]{:S(2)}) collective-permute-start(f32[6,66,1]{2,1,0:T(8,128)S(1)} %get-tuple-element.180), channel_id=1, source_target_pairs={{0,1},{1,2},{2,3},{3,4},{4,5},{5,6},{6,7},{8,9},{9,10},{10,11},{11... | collective-permute-start | bytes 4760 | tf_op jit(solution)/shard_map/while/body/eval_jaxpr/ppermute | solution.py:16
  426.8 24.8 %all-to-all-start = ((f32[64,1,192]{2,1,0:T(1,128)}), f32[64,1,192]{2,1,0:T(1,128)S(1)}, u32[]{:S(2)}, u32[]{:S(2)}) async-start(f32[64,1,192]{2,1,0:T(1,128)} %reshape.145), calls=%async_computation | async-start | bytes 131072 | tf_op jit(solution)/shard_map/while/body/eval_jaxpr/all_to_all | solution.py:42
  445.1 29.1 %collective-permute-start.2 = (f32[6,66,1]{2,1,0:T(8,128)S(1)}, f32[6,66,1]{2,1,0:T(8,128)S(1)}, u32[]{:S(2)}, u32[]{:S(2)}) collective-permute-start(f32[6,66,1]{2,1,0:T(8,128)S(1)} %get-tuple-element.180), channel_id=1, source_target_pairs={{0,1},{1,2},{2,3},{3,4},{4,5},{5,6},{6,7},{8,9},{9,10},{10,11},{11... | collective-permute-start | bytes 4760 | tf_op jit(solution)/shard_map/while/body/eval_jaxpr/ppermute | solution.py:16
  489.6 24.8 %all-to-all-start = ((f32[64,1,192]{2,1,0:T(1,128)}), f32[64,1,192]{2,1,0:T(1,128)S(1)}, u32[]{:S(2)}, u32[]{:S(2)}) async-start(f32[64,1,192]{2,1,0:T(1,128)} %reshape.145), calls=%async_computation | async-start | bytes 131072 | tf_op jit(solution)/shard_map/while/body/eval_jaxpr/all_to_all | solution.py:42
  507.8 29.1 %collective-permute-start.2 = (f32[6,66,1]{2,1,0:T(8,128)S(1)}, f32[6,66,1]{2,1,0:T(8,128)S(1)}, u32[]{:S(2)}, u32[]{:S(2)}) collective-permute-start(f32[6,66,1]{2,1,0:T(8,128)S(1)} %get-tuple-element.180), channel_id=1, source_target_pairs={{0,1},{1,2},{2,3},{3,4},{4,5},{5,6},{6,7},{8,9},{9,10},{10,11},{11... | collective-permute-start | bytes 4760 | tf_op jit(solution)/shard_map/while/body/eval_jaxpr/ppermute | solution.py:16
  570.5 29.1 %collective-permute-start.2 = (f32[6,66,1]{2,1,0:T(8,128)S(1)}, f32[6,66,1]{2,1,0:T(8,128)S(1)}, u32[]{:S(2)}, u32[]{:S(2)}) collective-permute-start(f32[6,66,1]{2,1,0:T(8,128)S(1)} %get-tuple-element.180), channel_id=1, source_target_pairs={{0,1},{1,2},{2,3},{3,4},{4,5},{5,6},{6,7},{8,9},{9,10},{10,11},{11... | collective-permute-start | bytes 4760 | tf_op jit(solution)/shard_map/while/body/eval_jaxpr/ppermute | solution.py:16
  633.2 29.1 %collective-permute-start.2 = (f32[6,66,1]{2,1,0:T(8,128)S(1)}, f32[6,66,1]{2,1,0:T(8,128)S(1)}, u32[]{:S(2)}, u32[]{:S(2)}) collective-permute-start(f32[6,66,1]{2,1,0:T(8,128)S(1)} %get-tuple-element.180), channel_id=1, source_target_pairs={{0,1},{1,2},{2,3},{3,4},{4,5},{5,6},{6,7},{8,9},{9,10},{10,11},{11... | collective-permute-start | bytes 4760 | tf_op jit(solution)/shard_map/while/body/eval_jaxpr/ppermute | solution.py:16
  677.7 24.8 %all-to-all-start = ((f32[64,1,192]{2,1,0:T(1,128)}), f32[64,1,192]{2,1,0:T(1,128)S(1)}, u32[]{:S(2)}, u32[]{:S(2)}) async-start(f32[64,1,192]{2,1,0:T(1,128)} %reshape.145), calls=%async_computation | async-start | bytes 131072 | tf_op jit(solution)/shard_map/while/body/eval_jaxpr/all_to_all | solution.py:42
  696.0 29.1 %collective-permute-start.2 = (f32[6,66,1]{2,1,0:T(8,128)S(1)}, f32[6,66,1]{2,1,0:T(8,128)S(1)}, u32[]{:S(2)}, u32[]{:S(2)}) collective-permute-start(f32[6,66,1]{2,1,0:T(8,128)S(1)} %get-tuple-element.180), channel_id=1, source_target_pairs={{0,1},{1,2},{2,3},{3,4},{4,5},{5,6},{6,7},{8,9},{9,10},{10,11},{11... | collective-permute-start | bytes 4760 | tf_op jit(solution)/shard_map/while/body/eval_jaxpr/ppermute | solution.py:16
  758.7 29.1 %collective-permute-start.2 = (f32[6,66,1]{2,1,0:T(8,128)S(1)}, f32[6,66,1]{2,1,0:T(8,128)S(1)}, u32[]{:S(2)}, u32[]{:S(2)}) collective-permute-start(f32[6,66,1]{2,1,0:T(8,128)S(1)} %get-tuple-element.180), channel_id=1, source_target_pairs={{0,1},{1,2},{2,3},{3,4},{4,5},{5,6},{6,7},{8,9},{9,10},{10,11},{11... | collective-permute-start | bytes 4760 | tf_op jit(solution)/shard_map/while/body/eval_jaxpr/ppermute | solution.py:16
  803.2 24.8 %all-to-all-start = ((f32[64,1,192]{2,1,0:T(1,128)}), f32[64,1,192]{2,1,0:T(1,128)S(1)}, u32[]{:S(2)}, u32[]{:S(2)}) async-start(f32[64,1,192]{2,1,0:T(1,128)} %reshape.145), calls=%async_computation | async-start | bytes 131072 | tf_op jit(solution)/shard_map/while/body/eval_jaxpr/all_to_all | solution.py:42
  821.4 29.1 %collective-permute-start.2 = (f32[6,66,1]{2,1,0:T(8,128)S(1)}, f32[6,66,1]{2,1,0:T(8,128)S(1)}, u32[]{:S(2)}, u32[]{:S(2)}) collective-permute-start(f32[6,66,1]{2,1,0:T(8,128)S(1)} %get-tuple-element.180), channel_id=1, source_target_pairs={{0,1},{1,2},{2,3},{3,4},{4,5},{5,6},{6,7},{8,9},{9,10},{10,11},{11... | collective-permute-start | bytes 4760 | tf_op jit(solution)/shard_map/while/body/eval_jaxpr/ppermute | solution.py:16
  884.1 29.1 %collective-permute-start.2 = (f32[6,66,1]{2,1,0:T(8,128)S(1)}, f32[6,66,1]{2,1,0:T(8,128)S(1)}, u32[]{:S(2)}, u32[]{:S(2)}) collective-permute-start(f32[6,66,1]{2,1,0:T(8,128)S(1)} %get-tuple-element.180), channel_id=1, source_target_pairs={{0,1},{1,2},{2,3},{3,4},{4,5},{5,6},{6,7},{8,9},{9,10},{10,11},{11... | collective-permute-start | bytes 4760 | tf_op jit(solution)/shard_map/while/body/eval_jaxpr/ppermute | solution.py:16
  946.8 29.1 %collective-permute-start.2 = (f32[6,66,1]{2,1,0:T(8,128)S(1)}, f32[6,66,1]{2,1,0:T(8,128)S(1)}, u32[]{:S(2)}, u32[]{:S(2)}) collective-permute-start(f32[6,66,1]{2,1,0:T(8,128)S(1)} %get-tuple-element.180), channel_id=1, source_target_pairs={{0,1},{1,2},{2,3},{3,4},{4,5},{5,6},{6,7},{8,9},{9,10},{10,11},{11... | collective-permute-start | bytes 4760 | tf_op jit(solution)/shard_map/while/body/eval_jaxpr/ppermute | solution.py:16
  991.3 24.8 %all-to-all-start = ((f32[64,1,192]{2,1,0:T(1,128)}), f32[64,1,192]{2,1,0:T(1,128)S(1)}, u32[]{:S(2)}, u32[]{:S(2)}) async-start(f32[64,1,192]{2,1,0:T(1,128)} %reshape.145), calls=%async_computation | async-start | bytes 131072 | tf_op jit(solution)/shard_map/while/body/eval_jaxpr/all_to_all | solution.py:42
  1009.6 29.1 %collective-permute-start.2 = (f32[6,66,1]{2,1,0:T(8,128)S(1)}, f32[6,66,1]{2,1,0:T(8,128)S(1)}, u32[]{:S(2)}, u32[]{:S(2)}) collective-permute-start(f32[6,66,1]{2,1,0:T(8,128)S(1)} %get-tuple-element.180), channel_id=1, source_target_pairs={{0,1},{1,2},{2,3},{3,4},{4,5},{5,6},{6,7},{8,9},{9,10},{10,11},{11... | collective-permute-start | bytes 4760 | tf_op jit(solution)/shard_map/while/body/eval_jaxpr/ppermute | solution.py:16
  1072.3 29.1 %collective-permute-start.2 = (f32[6,66,1]{2,1,0:T(8,128)S(1)}, f32[6,66,1]{2,1,0:T(8,128)S(1)}, u32[]{:S(2)}, u32[]{:S(2)}) collective-permute-start(f32[6,66,1]{2,1,0:T(8,128)S(1)} %get-tuple-element.180), channel_id=1, source_target_pairs={{0,1},{1,2},{2,3},{3,4},{4,5},{5,6},{6,7},{8,9},{9,10},{10,11},{11... | collective-permute-start | bytes 4760 | tf_op jit(solution)/shard_map/while/body/eval_jaxpr/ppermute | solution.py:16
  1135.0 29.1 %collective-permute-start.2 = (f32[6,66,1]{2,1,0:T(8,128)S(1)}, f32[6,66,1]{2,1,0:T(8,128)S(1)}, u32[]{:S(2)}, u32[]{:S(2)}) collective-permute-start(f32[6,66,1]{2,1,0:T(8,128)S(1)} %get-tuple-element.180), channel_id=1, source_target_pairs={{0,1},{1,2},{2,3},{3,4},{4,5},{5,6},{6,7},{8,9},{9,10},{10,11},{11... | collective-permute-start | bytes 4760 | tf_op jit(solution)/shard_map/while/body/eval_jaxpr/ppermute | solution.py:16
  1179.5 24.8 %all-to-all-start = ((f32[64,1,192]{2,1,0:T(1,128)}), f32[64,1,192]{2,1,0:T(1,128)S(1)}, u32[]{:S(2)}, u32[]{:S(2)}) async-start(f32[64,1,192]{2,1,0:T(1,128)} %reshape.145), calls=%async_computation | async-start | bytes 131072 | tf_op jit(solution)/shard_map/while/body/eval_jaxpr/all_to_all | solution.py:42
  1197.7 29.1 %collective-permute-start.2 = (f32[6,66,1]{2,1,0:T(8,128)S(1)}, f32[6,66,1]{2,1,0:T(8,128)S(1)}, u32[]{:S(2)}, u32[]{:S(2)}) collective-permute-start(f32[6,66,1]{2,1,0:T(8,128)S(1)} %get-tuple-element.180), channel_id=1, source_target_pairs={{0,1},{1,2},{2,3},{3,4},{4,5},{5,6},{6,7},{8,9},{9,10},{10,11},{11... | collective-permute-start | bytes 4760 | tf_op jit(solution)/shard_map/while/body/eval_jaxpr/ppermute | solution.py:16
  1260.4 29.1 %collective-permute-start.2 = (f32[6,66,1]{2,1,0:T(8,128)S(1)}, f32[6,66,1]{2,1,0:T(8,128)S(1)}, u32[]{:S(2)}, u32[]{:S(2)}) collective-permute-start(f32[6,66,1]{2,1,0:T(8,128)S(1)} %get-tuple-element.180), channel_id=1, source_target_pairs={{0,1},{1,2},{2,3},{3,4},{4,5},{5,6},{6,7},{8,9},{9,10},{10,11},{11... | collective-permute-start | bytes 4760 | tf_op jit(solution)/shard_map/while/body/eval_jaxpr/ppermute | solution.py:16
  (159 other events, 4205.3 us)
